TPU v7x, 256 devices: a whole 4x4x8 slice. The times are simulated.
256 devices in a mesh: grp: 8 (over y, core), dev: 32 (over z, x).
Axes of the slice: x: 4, y: 4, z: 8, core: 2. Of those that a mesh axis runs over, the one named last changes fastest.
Arguments:
- objective: float32 [8, 32, 1024, 256], P('grp', 'dev'), may hold values from -24 to 24
- schur: float32 [8, 32, 1024, 1024], P('grp', 'dev')
- local_inverse: float32 [8, 32, 1024, 1024], P('grp', 'dev')
- coarse_basis: float32 [8, 32, 64, 1024], P('grp', 'dev'), may hold values from -0.09375 to 0.09375
- coarse_inverse: float32 [8, 32, 32, 8192], P(None, 'dev', None, 'grp')
- stiffness: int32 [8, 32, 1024], P('grp', 'dev'), may hold values from 1 to 8
- face_rows: int32 [8, 32, 4, 256], P('grp', 'dev'), may hold values from -1 to 1023, as said below
- coarse_map: int32 [8, 32, 64], P('grp', 'dev'), may hold values from 0 to 255
Outputs:
- adjoint: float32 [8, 32, 1024, 256], P('grp', 'dev')
Inputs may be any that keep to these rules, and one draw needn't show every extreme that they name: `face_rows`: slot k of face p names the local row of the k-th row that the subdomain shares with its neighbour across face p, or -1; the live slots of a face come first, and the neighbour lists the same shared rows in the same order in its opposite face. The live slots of a subdomain name its rows 0 to n - 1 once each, n at most 1024, and at least one subdomain has all 1024 rows. Faces at the ends of the layout are empty; a face that joins two subdomains has 1 to 256 rows. `coarse_map`: entry e of subdomain (g, d) names the coarse dof (e // 32, d, e % 32), owned by the subdomain at grp index e // 32 of the same dev index.
All inputs are finite; a program needn't handle non-finite values.
Results may differ from a plain program's by a relative error of at most 0.0003.
Values sent between devices are 32-bit elements; how exact they have to be, the bound alone decides.
No kernel may reach another device: no remote copies, remote signals or barrier semaphores. Data moves between devices by JAX's collectives and lax.ppermute only.
A program may use at most 64 MiB of HBM per device.

v0:
```python
import jax
import jax.numpy as jnp
from jax import lax
from jax.sharding import PartitionSpec as P

INTERFACE = 1024
FACE_ROWS = 256
OWNED = 32
SWEEPS = 2


def padded(value, sides, width):
    for axis, dim in sides:
        size, length = (lax.axis_size(axis), value.shape[dim])
        up = [(i, (i + 1) % size) for i in range(size - 1)]
        down = [(j, i) for i, j in up]
        last = lax.slice_in_dim(value, length - width, length, axis=dim)
        initial = lax.slice_in_dim(value, 0, width, axis=dim)
        before = lax.ppermute(last, axis, up)
        after = lax.ppermute(initial, axis, down)
        value = jnp.concatenate([before, value, after], axis=dim)
    return value


def contract_first(left, right):
    return lax.dot_general(
        left,
        right,
        (((0,), (0,)), ((), ())),
        precision=lax.Precision.HIGHEST,
        preferred_element_type=jnp.float32,
    )


def on_device(
    objective, schur, local_inverse, coarse_basis, coarse_inverse, stiffness, face_rows, coarse_map
):
    highest = lax.Precision.HIGHEST
    schur_block = schur[0, 0]
    local_block = local_inverse[0, 0]
    basis_rows = coarse_basis[0, 0]
    inverse_tile = coarse_inverse.reshape(-1, coarse_inverse.shape[3])
    slot_rows = face_rows[0, 0]
    local_map = coarse_map[0, 0]
    gradient = objective[0, 0]
    slot_count = 4 * FACE_ROWS
    slot_index = jnp.where(slot_rows < 0, INTERFACE, slot_rows).reshape(-1)
    empty_map = jnp.full((INTERFACE,), slot_count, jnp.int32)
    inverse = empty_map.at[slot_index].set(jnp.arange(slot_count, dtype=jnp.int32), mode="drop")
    live_rows = (inverse < slot_count).astype(jnp.float32)[:, None]

    def neighbour(values):
        packed = jnp.take(values, slot_index, axis=0, mode="fill", fill_value=0)
        packed = packed.reshape(4, FACE_ROWS, values.shape[-1])
        packet = jnp.stack([jnp.stack([packed[2], packed[1]]), jnp.stack([packed[0], packed[3]])])
        extended = padded(packet, (("grp", 0), ("dev", 1)), 1)
        received = jnp.stack([extended[1, 0], extended[2, 3], extended[0, 2], extended[3, 1]])
        received = received.reshape(slot_count, values.shape[-1])
        return jnp.take(received, inverse, axis=0, mode="fill", fill_value=0)

    multiplicity = stiffness[0, 0].astype(jnp.float32)[:, None]
    weight = live_rows * multiplicity / (multiplicity + neighbour(multiplicity))
    column_rows = inverse_tile.shape[0]
    onehot = (local_map[:, None] == jnp.arange(column_rows, dtype=jnp.int32)[None, :]).astype(
        jnp.float32
    )
    dev_position = lax.axis_index("dev")
    adjoint = jnp.zeros(gradient.shape, jnp.float32)
    for sweep_index in range(SWEEPS):
        if sweep_index == 0:
            remain = gradient
        else:
            remain = gradient - contract_first(schur_block, adjoint)
        residual = live_rows * (remain + neighbour(remain))
        weighted = weight * residual
        local_terms = jnp.dot(
            basis_rows, weighted, precision=highest, preferred_element_type=jnp.float32
        )
        spread_terms = contract_first(onehot, local_terms)
        column_residual = lax.psum(spread_terms, "grp")
        partial_sums = contract_first(inverse_tile, column_residual)
        summed = lax.psum(partial_sums, "dev")
        owned_part = lax.dynamic_slice_in_dim(summed, dev_position * OWNED, OWNED, 0)
        column_solution = lax.all_gather(owned_part, "grp", axis=0, tiled=True)
        local_solution = jnp.dot(
            onehot, column_solution, precision=highest, preferred_element_type=jnp.float32
        )
        correction = contract_first(basis_rows, local_solution)
        update = weight * (contract_first(local_block, weighted) + correction)
        adjoint = adjoint + update + neighbour(update)
    return adjoint[None, None]


def solution(mesh):
    return jax.shard_map(
        on_device,
        mesh=mesh,
        in_specs=(
            P("grp", "dev", None, None),
            P("grp", "dev", None, None),
            P("grp", "dev", None, None),
            P("grp", "dev", None, None),
            P(None, "dev", None, "grp"),
            P("grp", "dev", None),
            P("grp", "dev", None, None),
            P("grp", "dev", None),
        ),
        out_specs=P("grp", "dev", None, None),
        check_vma=False,
    )
```

profile of v0, /device:TPU:14, one launch (start us, length us, event | category | flops | bytes accessed | tf_op | source)
XLA Modules:
  0.0 766.2 jit_solution(6774467022367490812)
XLA Ops:
  8.0 4.5 gather_fusion
  27.5 4.3 scatter_custom_fusion
  41.0 5.8 collective-permute-start.6
  46.9 4.5 gather_fusion.1
  55.4 15.2 %collective-permute-done.6 = f32[4,1,256,256]{3,2,1,0:T(8,128)} collective-permute-done((f32[4,1,256,256]{3,2,1,0:T(8,128)}, f32[4,1,256,256]{3,2,1,0:T(8,128)}, u32[]{:S(2)}, u32[]{:S(2)}) %collective-permute-start.6) | collective-permute-done | bytes 1048608 | tf_op jit(solution)/shard_map/ppermute | solution.py:19
  71.5 9.8 %collective-permute-done.7 = f32[4,1,256,256]{3,2,1,0:T(8,128)S(1)} collective-permute-done((f32[4,1,256,256]{3,2,1,0:T(8,128)S(1)}, f32[4,1,256,256]{3,2,1,0:T(8,128)S(1)}, u32[]{:S(2)}, u32[]{:S(2)}) %collective-permute-start.7) | collective-permute-done | bytes 1048608 | tf_op jit(solution)/shard_map/ppermute | solution.py:20
  81.4 4.7 gather_fusion.3
  90.1 66.4 %all-reduce.5.cloned.1.call-done = f32[256,256]{1,0:T(8,128)} async-done(((f32[256,256]{1,0:T(8,128)}), f32[256,256]{1,0:T(8,128)}) %all-reduce.5.cloned.1.call-update) | async-done | bytes 262160 | tf_op jit(solution)/shard_map/psum | solution.py:80
  159.5 150.0 %all-reduce.7.cloned.1.call-done = f32[1024,256]{0,1:T(8,128)} async-done(((f32[1024,256]{0,1:T(8,128)}), f32[1024,256]{0,1:T(8,128)}) %all-reduce.7.cloned.1.call-update) | async-done | bytes 1048592 | tf_op jit(solution)/shard_map/psum | solution.py:82
  311.2 13.3 %all_gather.6 = f32[256,256]{1,0:T(8,128)S(1)} all-gather(f32[32,256]{1,0:T(8,128)} %copy.36), channel_id=1, replica_groups=mesh['grp'=8,'dev'=32] {'grp'}, dimensions={0}, use_global_device_ids=true | all-gather | bytes 294912 | tf_op jit(solution)/shard_map/all_gather | solution.py:84
  326.4 6.9 fusion.12
  334.9 4.7 gather_fusion.4
  345.8 4.7 collective-permute-done.9
  360.6 19.8 %collective-permute-done.10 = f32[4,1,256,256]{3,2,1,0:T(8,128)S(1)} collective-permute-done((f32[4,1,256,256]{3,2,1,0:T(8,128)S(1)}, f32[4,1,256,256]{3,2,1,0:T(8,128)S(1)}, u32[]{:S(2)}, u32[]{:S(2)}) %collective-permute-start.10) | collective-permute-done | bytes 1048608 | tf_op jit(solution)/shard_map/ppermute | solution.py:19
  380.4 5.8 collective-permute-done.11
  386.4 4.7 gather_fusion.5
  393.6 6.4 fusion.27
  400.4 4.7 gather_fusion.6
  411.0 4.2 collective-permute-done.13
  421.3 4.1 collective-permute-start.15
  425.5 19.1 %collective-permute-done.14 = f32[4,1,256,256]{3,2,1,0:T(8,128)S(1)} collective-permute-done((f32[4,1,256,256]{3,2,1,0:T(8,128)S(1)}, f32[4,1,256,256]{3,2,1,0:T(8,128)S(1)}, u32[]{:S(2)}, u32[]{:S(2)}) %collective-permute-start.14) | collective-permute-done | bytes 1048608 | tf_op jit(solution)/shard_map/ppermute | solution.py:19
  444.6 4.0 collective-permute-done.15
  448.7 4.7 gather_fusion.7
  457.3 62.6 %all-reduce.9.cloned.1.call-done = f32[256,256]{1,0:T(8,128)} async-done(((f32[256,256]{1,0:T(8,128)}), f32[256,256]{1,0:T(8,128)}) %all-reduce.9.cloned.1.call-update) | async-done | bytes 262160 | tf_op jit(solution)/shard_map/psum | solution.py:80
  523.0 149.5 %all-reduce.11.cloned.1.call-done = f32[1024,256]{0,1:T(8,128)} async-done(((f32[1024,256]{0,1:T(8,128)}), f32[1024,256]{0,1:T(8,128)}) %all-reduce.11.cloned.1.call-update) | async-done | bytes 1048592 | tf_op jit(solution)/shard_map/psum | solution.py:82
  674.1 13.1 %all_gather.7 = f32[256,256]{1,0:T(8,128)S(1)} all-gather(f32[32,256]{1,0:T(8,128)} %copy.41), channel_id=1, replica_groups=mesh['grp'=8,'dev'=32] {'grp'}, dimensions={0}, use_global_device_ids=true | all-gather | bytes 294912 | tf_op jit(solution)/shard_map/all_gather | solution.py:84
  689.2 6.9 fusion.21
  706.2 4.7 collective-permute-done.17
  715.0 4.0 collective-permute-start.18
  721.1 19.8 %collective-permute-done.18 = f32[4,1,256,256]{3,2,1,0:T(8,128)S(1)} collective-permute-done((f32[4,1,256,256]{3,2,1,0:T(8,128)S(1)}, f32[4,1,256,256]{3,2,1,0:T(8,128)S(1)}, u32[]{:S(2)}, u32[]{:S(2)}) %collective-permute-start.18) | collective-permute-done | bytes 1048608 | tf_op jit(solution)/shard_map/ppermute | solution.py:19
  740.8 5.8 collective-permute-done.19
  746.8 4.6 gather_fusion.9
  (155 shorter events, 108.7 us)
Async XLA Ops:
  6.5 149.9 %copy-start = (f32[8,1,32,1024]{3,2,1,0:T(8,128)S(1)}, f32[8,1,32,1024]{3,2,1,0:T(8,128)}, u32[]{:S(2)}) copy-start(f32[8,1,32,1024]{3,2,1,0:T(8,128)} %param.16) | copy-start | bytes 3145732
  6.5 149.9 %all-reduce.5.cloned.1.call-start = ((), (), s32[]{:S(2)}) async-start(), calls=%async_computation | async-start | bytes 524288 | tf_op jit(solution)/shard_map/psum | solution.py:80
  8.0 8.9 %copy-start.1 = (f32[1,1,1024,256]{3,2,1,0:T(8,128)S(1)}, f32[1,1,1024,256]{3,2,1,0:T(8,128)}, u32[]{:S(2)}) copy-start(f32[1,1,1024,256]{3,2,1,0:T(8,128)} %param.12) | copy-start | bytes 3145732
  12.6 7.9 %copy-start.8 = (pred[1024]{0:T(1024)(128)(4,1)}, pred[1024]{0:T(1024)(128)(4,1)S(1)}, u32[]{:S(2)}) copy-start(pred[1024]{0:T(1024)(128)(4,1)S(1)} %get-tuple-element.10) | copy-start | bytes 3076
  12.6 19.6 %collective-permute-start.1 = (f32[1,2,256,1]{2,1,3,0:T(2,128)S(1)}, f32[1,2,256,1]{2,1,3,0:T(2,128)S(1)}, u32[]{:S(2)}, u32[]{:S(2)}) collective-permute-start(f32[1,2,256,1]{2,1,3,0:T(2,128)S(1)} %maximum_bitcast_fusion.9), channel_id=1, source_target_pairs={{32,0},{64,32},{96,64},{128,96},{160,128},{192,160},{224,192},{33,... | collective-permute-start | bytes 6152 | tf_op jit(solution)/shard_map/ppermute | solution.py:20
  14.5 17.7 %collective-permute-start = (f32[1,2,256,1]{2,1,3,0:T(2,128)S(1)}, f32[1,2,256,1]{2,1,3,0:T(2,128)S(1)}, u32[]{:S(2)}, u32[]{:S(2)}) collective-permute-start(f32[1,2,256,1]{2,1,3,0:T(2,128)S(1)} %maximum_bitcast_fusion.8), channel_id=1, source_target_pairs={{0,32},{32,64},{64,96},{96,128},{128,160},{160,192},{192,224},{1,3... | collective-permute-start | bytes 6152 | tf_op jit(solution)/shard_map/ppermute | solution.py:19
  20.7 6.8 copy-start.11
  21.6 16.6 %collective-permute-start.5 = (f32[1,2,256,256]{3,2,1,0:T(8,128)}, f32[1,2,256,256]{3,2,1,0:T(8,128)}, u32[]{:S(2)}, u32[]{:S(2)}) collective-permute-start(f32[1,2,256,256]{3,2,1,0:T(8,128)} %maximum_bitcast_fusion.1), channel_id=1, source_target_pairs={{32,0},{64,32},{96,64},{128,96},{160,128},{192,160},{224,192},{33,... | collective-permute-start | bytes 1572872 | tf_op jit(solution)/shard_map/ppermute | solution.py:20
  25.6 12.6 %collective-permute-start.4 = (f32[1,2,256,256]{3,2,1,0:T(8,128)}, f32[1,2,256,256]{3,2,1,0:T(8,128)}, u32[]{:S(2)}, u32[]{:S(2)}) collective-permute-start(f32[1,2,256,256]{3,2,1,0:T(8,128)} %maximum_bitcast_fusion), channel_id=1, source_target_pairs={{0,32},{32,64},{64,96},{96,128},{128,160},{160,192},{192,224},{1,3... | collective-permute-start | bytes 1572872 | tf_op jit(solution)/shard_map/ppermute | solution.py:19
  32.3 5.9 collective-permute-start.2
  36.0 10.8 %collective-permute-start.3 = (f32[4,1,256,1]{2,1,3,0:T(1,128)S(1)}, f32[4,1,256,1]{2,1,3,0:T(1,128)S(1)}, u32[]{:S(2)}, u32[]{:S(2)}) collective-permute-start(f32[4,1,256,1]{2,1,3,0:T(1,128)S(1)} %get-tuple-element.38), channel_id=1, source_target_pairs={{1,0},{2,1},{3,2},{4,3},{5,4},{6,5},{7,6},{8,7},{9,8},{10,9},{11,1... | collective-permute-start | bytes 12296 | tf_op jit(solution)/shard_map/ppermute | solution.py:20
  41.0 29.5 %collective-permute-start.6 = (f32[4,1,256,256]{3,2,1,0:T(8,128)}, f32[4,1,256,256]{3,2,1,0:T(8,128)}, u32[]{:S(2)}, u32[]{:S(2)}) collective-permute-start(f32[4,1,256,256]{3,2,1,0:T(8,128)} %get-tuple-element.19), channel_id=1, source_target_pairs={{0,1},{1,2},{2,3},{3,4},{4,5},{5,6},{6,7},{7,8},{8,9},{9,10},{10,1... | collective-permute-start | bytes 3145736 | tf_op jit(solution)/shard_map/ppermute | solution.py:19
  46.9 6.5 copy-start.12
  51.4 29.9 %collective-permute-start.7 = (f32[4,1,256,256]{3,2,1,0:T(8,128)S(1)}, f32[4,1,256,256]{3,2,1,0:T(8,128)S(1)}, u32[]{:S(2)}, u32[]{:S(2)}) collective-permute-start(f32[4,1,256,256]{3,2,1,0:T(8,128)S(1)} %get-tuple-element.20), channel_id=1, source_target_pairs={{1,0},{2,1},{3,2},{4,3},{5,4},{6,5},{7,6},{8,7},{9,8},{10,9},{11,1... | collective-permute-start | bytes 3145736 | tf_op jit(solution)/shard_map/ppermute | solution.py:20
  53.4 34.4 %copy-start.5 = (pred[1024]{0:T(1024)(128)(4,1)}, pred[1024]{0:T(1024)(128)(4,1)S(1)}, u32[]{:S(2)}) copy-start(pred[1024]{0:T(1024)(128)(4,1)S(1)} %get-tuple-element.8) | copy-start | bytes 3076
  90.0 219.4 %all-reduce.7.cloned.1.call-start = ((), (), s32[]{:S(2)}) async-start(), calls=%async_computation.1 | async-start | bytes 2097152 | tf_op jit(solution)/shard_map/psum | solution.py:82
  159.4 360.6 %all-reduce.9.cloned.1.call-start = ((), (), s32[]{:S(2)}) async-start(), calls=%async_computation.2 | async-start | bytes 524288 | tf_op jit(solution)/shard_map/psum | solution.py:80
  334.9 4.7 copy-start.9
  341.1 9.4 %collective-permute-start.9 = (f32[1,2,256,256]{3,2,1,0:T(8,128)S(1)}, f32[1,2,256,256]{3,2,1,0:T(8,128)S(1)}, u32[]{:S(2)}, u32[]{:S(2)}) collective-permute-start(f32[1,2,256,256]{3,2,1,0:T(8,128)S(1)} %maximum_bitcast_fusion.3), channel_id=1, source_target_pairs={{32,0},{64,32},{96,64},{128,96},{160,128},{192,160},{224,192},{33,... | collective-permute-start | bytes 1572872 | tf_op jit(solution)/shard_map/ppermute | solution.py:20
  343.9 10.5 %collective-permute-start.8 = (f32[1,2,256,256]{3,2,1,0:T(8,128)S(1)}, f32[1,2,256,256]{3,2,1,0:T(8,128)S(1)}, u32[]{:S(2)}, u32[]{:S(2)}) collective-permute-start(f32[1,2,256,256]{3,2,1,0:T(8,128)S(1)} %maximum_bitcast_fusion.2), channel_id=1, source_target_pairs={{0,32},{32,64},{64,96},{96,128},{128,160},{160,192},{192,224},{1,3... | collective-permute-start | bytes 1572872 | tf_op jit(solution)/shard_map/ppermute | solution.py:19
  354.6 25.8 %collective-permute-start.10 = (f32[4,1,256,256]{3,2,1,0:T(8,128)S(1)}, f32[4,1,256,256]{3,2,1,0:T(8,128)S(1)}, u32[]{:S(2)}, u32[]{:S(2)}) collective-permute-start(f32[4,1,256,256]{3,2,1,0:T(8,128)S(1)} %get-tuple-element.17), channel_id=1, source_target_pairs={{0,1},{1,2},{2,3},{3,4},{4,5},{5,6},{6,7},{7,8},{8,9},{9,10},{10,1... | collective-permute-start | bytes 3145736 | tf_op jit(solution)/shard_map/ppermute | solution.py:19
  358.7 27.6 %collective-permute-start.11 = (f32[4,1,256,256]{3,2,1,0:T(8,128)S(1)}, f32[4,1,256,256]{3,2,1,0:T(8,128)S(1)}, u32[]{:S(2)}, u32[]{:S(2)}) collective-permute-start(f32[4,1,256,256]{3,2,1,0:T(8,128)S(1)} %get-tuple-element.18), channel_id=1, source_target_pairs={{1,0},{2,1},{3,2},{4,3},{5,4},{6,5},{7,6},{8,7},{9,8},{10,9},{11,1... | collective-permute-start | bytes 3145736 | tf_op jit(solution)/shard_map/ppermute | solution.py:20
  406.6 8.6 %collective-permute-start.13 = (f32[1,2,256,256]{3,2,1,0:T(8,128)S(1)}, f32[1,2,256,256]{3,2,1,0:T(8,128)S(1)}, u32[]{:S(2)}, u32[]{:S(2)}) collective-permute-start(f32[1,2,256,256]{3,2,1,0:T(8,128)S(1)} %maximum_bitcast_fusion.5), channel_id=1, source_target_pairs={{32,0},{64,32},{96,64},{128,96},{160,128},{192,160},{224,192},{33,... | collective-permute-start | bytes 1572872 | tf_op jit(solution)/shard_map/ppermute | solution.py:20
  408.6 10.5 %collective-permute-start.12 = (f32[1,2,256,256]{3,2,1,0:T(8,128)S(1)}, f32[1,2,256,256]{3,2,1,0:T(8,128)S(1)}, u32[]{:S(2)}, u32[]{:S(2)}) collective-permute-start(f32[1,2,256,256]{3,2,1,0:T(8,128)S(1)} %maximum_bitcast_fusion.4), channel_id=1, source_target_pairs={{0,32},{32,64},{64,96},{96,128},{128,160},{160,192},{192,224},{1,3... | collective-permute-start | bytes 1572872 | tf_op jit(solution)/shard_map/ppermute | solution.py:19
  419.3 25.3 %collective-permute-start.14 = (f32[4,1,256,256]{3,2,1,0:T(8,128)S(1)}, f32[4,1,256,256]{3,2,1,0:T(8,128)S(1)}, u32[]{:S(2)}, u32[]{:S(2)}) collective-permute-start(f32[4,1,256,256]{3,2,1,0:T(8,128)S(1)} %get-tuple-element.15), channel_id=1, source_target_pairs={{0,1},{1,2},{2,3},{3,4},{4,5},{5,6},{6,7},{7,8},{8,9},{9,10},{10,1... | collective-permute-start | bytes 3145736 | tf_op jit(solution)/shard_map/ppermute | solution.py:19
  421.3 27.4 %collective-permute-start.15 = (f32[4,1,256,256]{3,2,1,0:T(8,128)S(1)}, f32[4,1,256,256]{3,2,1,0:T(8,128)S(1)}, u32[]{:S(2)}, u32[]{:S(2)}) collective-permute-start(f32[4,1,256,256]{3,2,1,0:T(8,128)S(1)} %get-tuple-element.16), channel_id=1, source_target_pairs={{1,0},{2,1},{3,2},{4,3},{5,4},{6,5},{7,6},{8,7},{9,8},{10,9},{11,1... | collective-permute-start | bytes 3145736 | tf_op jit(solution)/shard_map/ppermute | solution.py:20
  457.3 215.2 %all-reduce.11.cloned.1.call-start = ((), (), s32[]{:S(2)}) async-start(), calls=%async_computation.3 | async-start | bytes 2097152 | tf_op jit(solution)/shard_map/psum | solution.py:82
  701.5 9.4 %collective-permute-start.17 = (f32[1,2,256,256]{3,2,1,0:T(8,128)S(1)}, f32[1,2,256,256]{3,2,1,0:T(8,128)S(1)}, u32[]{:S(2)}, u32[]{:S(2)}) collective-permute-start(f32[1,2,256,256]{3,2,1,0:T(8,128)S(1)} %maximum_bitcast_fusion.7), channel_id=1, source_target_pairs={{32,0},{64,32},{96,64},{128,96},{160,128},{192,160},{224,192},{33,... | collective-permute-start | bytes 1572872 | tf_op jit(solution)/shard_map/ppermute | solution.py:20
  704.3 10.5 %collective-permute-start.16 = (f32[1,2,256,256]{3,2,1,0:T(8,128)S(1)}, f32[1,2,256,256]{3,2,1,0:T(8,128)S(1)}, u32[]{:S(2)}, u32[]{:S(2)}) collective-permute-start(f32[1,2,256,256]{3,2,1,0:T(8,128)S(1)} %maximum_bitcast_fusion.6), channel_id=1, source_target_pairs={{0,32},{32,64},{64,96},{96,128},{128,160},{160,192},{192,224},{1,3... | collective-permute-start | bytes 1572872 | tf_op jit(solution)/shard_map/ppermute | solution.py:19
  715.0 25.8 %collective-permute-start.18 = (f32[4,1,256,256]{3,2,1,0:T(8,128)S(1)}, f32[4,1,256,256]{3,2,1,0:T(8,128)S(1)}, u32[]{:S(2)}, u32[]{:S(2)}) collective-permute-start(f32[4,1,256,256]{3,2,1,0:T(8,128)S(1)} %get-tuple-element.13), channel_id=1, source_target_pairs={{0,1},{1,2},{2,3},{3,4},{4,5},{5,6},{6,7},{7,8},{8,9},{9,10},{10,1... | collective-permute-start | bytes 3145736 | tf_op jit(solution)/shard_map/ppermute | solution.py:19
  719.1 27.6 %collective-permute-start.19 = (f32[4,1,256,256]{3,2,1,0:T(8,128)S(1)}, f32[4,1,256,256]{3,2,1,0:T(8,128)S(1)}, u32[]{:S(2)}, u32[]{:S(2)}) collective-permute-start(f32[4,1,256,256]{3,2,1,0:T(8,128)S(1)} %get-tuple-element.14), channel_id=1, source_target_pairs={{1,0},{2,1},{3,2},{4,3},{5,4},{6,5},{7,6},{8,7},{9,8},{10,9},{11,1... | collective-permute-start | bytes 3145736 | tf_op jit(solution)/shard_map/ppermute | solution.py:20
  746.8 7.4 copy-start.7
  (7 other events, 18.6 us)
Sparse Core Ops, SparseCore 0:
  90.1 66.2 all-reduce.4
  160.3 149.1 all-reduce.6
  457.4 62.5 all-reduce.8
  523.3 149.1 all-reduce.10
where the time goes:
time: 767 us; the launch traced here: 766 us
  waiting for transfers between devices  553 us (72%)
  local copies, waits for them, and re-layouts  72.2 us (9%)
  starting transfers between devices  54.6 us (7%)
  matrix products  34.6 us (5%)
  blocking collectives  26.3 us (3%)
  between operations  14 us (2%)
  other arithmetic  11.2 us (1%)
    psum x2, waiting for transfers between devices, on_device(): summed = lax.psum(partial_sums, 'dev')  300 us
    psum x2, waiting for transfers between devices, on_device(): column_residual = lax.psum(spread_terms, 'grp')  129 us
    ppermute x10, waiting for transfers between devices, padded(): before = lax.ppermute(last, axis, up)  85.5 us
    ppermute x10, waiting for transfers between devices, padded(): after = lax.ppermute(initial, axis, down)  39.2 us
    gather x9, local copies, waits for them, and re-layouts, neighbour(): return jnp.take(received, inverse, axis=0, mode='fill', fill_value=0)  31.6 us
    dot_general x9, matrix products, contract_first(): lax.dot_general(left, right, (((0,), (0,)), ((), ())), precision=lax.Prec...  30.5 us
    ppermute x10, starting transfers between devices, padded(): before = lax.ppermute(last, axis, up)  30.1 us
    all_gather x2, blocking collectives, on_device(): column_solution = lax.all_gather(owned_part, 'grp', axis=0, tiled=True)  26.3 us
  transfers between devices with their start and end apart: 24, of which 18 were waited for; matrix products, arithmetic and copies ran while one was open for 3% of the time, Pallas kernels for 0%

commit v1 on v0

--- a/solution.py
+++ b/solution.py
@@ -7,6 +7,28 @@
 FACE_ROWS = 256
 OWNED = 32
 SWEEPS = 2
+
+
+def laid_out(tiles, dim):
+    tiles = jnp.moveaxis(tiles, 0, dim)
+    shape = tiles.shape
+    return tiles.reshape(*shape[:dim], shape[dim] * shape[dim + 1], *shape[dim + 2 :])
+
+
+def collect(shard, axis, dim):
+    size = lax.axis_size(axis)
+    pairs = [(i, (i + 1) % size) for i in range(size)]
+    back = [(b, a) for a, b in pairs]
+    lower, upper = ([], [])
+    for lap in range(size - 1):
+        if lap % 2 == 0:
+            lower.append(lax.ppermute(lower[-1] if lower else shard, axis, pairs))
+        else:
+            upper.append(lax.ppermute(upper[-1] if upper else shard, axis, back))
+    tiles = jnp.stack([*lower[::-1], shard, *upper])
+    shift = lax.axis_index(axis) - len(lower)
+    tiles = tiles[(jnp.arange(size) - shift) % size]
+    return laid_out(tiles, dim)
 
 
 def padded(value, sides, width):
@@ -81,7 +103,7 @@
         partial_sums = contract_first(inverse_tile, column_residual)
         summed = lax.psum(partial_sums, "dev")
         owned_part = lax.dynamic_slice_in_dim(summed, dev_position * OWNED, OWNED, 0)
-        column_solution = lax.all_gather(owned_part, "grp", axis=0, tiled=True)
+        column_solution = collect(owned_part, "grp", 0)
         local_solution = jnp.dot(
             onehot, column_solution, precision=highest, preferred_element_type=jnp.float32
         )

time: 767 us -> 813 us (1.060)
  local copies, waits for them, and re-layouts: 72.2 us -> 112 us
  blocking collectives: 26.3 us -> 0 us
  waiting for transfers between devices: 553 us -> 572 us
  starting transfers between devices: 54.6 us -> 64.6 us
    all_gather x2 -> x0, blocking collectives: 26.3 us -> none  [on_device(): column_solution = lax.all_gather(owned_part, 'grp', axis=0, tiled=True)]
    another operation x0 -> x16, local copies, waits for them, and re-layouts: none -> 18.6 us  [collect(): tiles = jnp.stack([*lower[::-1], shard, *upper])]
    unnamed x33 -> x51, local copies, waits for them, and re-layouts: 1.18 us -> 17.8 us
    ppermute x0 -> x14, waiting for transfers between devices: none -> 16.1 us  [the longest x8 16.1 us: collect(): lower.append(lax.ppermute(lower[-1] if lower else shard, axis, pairs))]
    ppermute x0 -> x14, starting transfers between devices: none -> 9.8 us  [the longest x6 9.74 us: collect(): upper.append(lax.ppermute(upper[-1] if upper else shard, axis, back))]
  transfers between devices with their start and end apart: 24 -> 38, of which waited for: 18 -> 25; matrix products, arithmetic and copies ran while one was open for 3% -> 4% of each run, Pallas kernels for 0% -> 0%
where the time goes in v1:
time: 813 us; the launch traced here: 810 us
  waiting for transfers between devices  572 us (70%)
  local copies, waits for them, and re-layouts  112 us (14%)
  starting transfers between devices  64.6 us (8%)
  matrix products  35.3 us (4%)
  between operations  14.1 us (2%)
  other arithmetic  11.8 us (1%)
    psum x2, waiting for transfers between devices, on_device(): summed = lax.psum(partial_sums, 'dev')  299 us
    psum x2, waiting for transfers between devices, on_device(): column_residual = lax.psum(spread_terms, 'grp')  129 us
    ppermute x10, waiting for transfers between devices, padded(): before = lax.ppermute(last, axis, up)  88.8 us
    ppermute x10, waiting for transfers between devices, padded(): after = lax.ppermute(initial, axis, down)  38.8 us
    gather x9, local copies, waits for them, and re-layouts, neighbour(): return jnp.take(received, inverse, axis=0, mode='fill', fill_value=0)  31.7 us
    dot_general x9, matrix products, contract_first(): lax.dot_general(left, right, (((0,), (0,)), ((), ())), precision=lax.Prec...  30.5 us
    ppermute x10, starting transfers between devices, padded(): before = lax.ppermute(last, axis, up)  28 us
    ppermute x10, starting transfers between devices, padded(): after = lax.ppermute(initial, axis, down)  26.5 us
  transfers between devices with their start and end apart: 38, of which 25 were waited for; matrix products, arithmetic and copies ran while one was open for 4% of the time, Pallas kernels for 0%

profile of v1, /device:TPU:14, one launch (start us, length us, event | category | flops | bytes accessed | tf_op | source)
XLA Modules:
  0.0 810.3 jit_solution(1196477420385084129)
XLA Ops:
  8.7 4.3 scatter_custom_fusion
  13.1 4.5 gather_fusion.2
  48.0 4.5 gather_fusion.3
  56.7 14.8 %collective-permute-done.6 = f32[4,1,256,256]{3,2,1,0:T(8,128)} collective-permute-done((f32[4,1,256,256]{3,2,1,0:T(8,128)}, f32[4,1,256,256]{3,2,1,0:T(8,128)}, u32[]{:S(2)}, u32[]{:S(2)}) %collective-permute-start.6) | collective-permute-done | bytes 1048608 | tf_op jit(solution)/shard_map/ppermute | solution.py:41
  72.5 9.5 %collective-permute-done.7 = f32[4,1,256,256]{3,2,1,0:T(8,128)S(1)} collective-permute-done((f32[4,1,256,256]{3,2,1,0:T(8,128)S(1)}, f32[4,1,256,256]{3,2,1,0:T(8,128)S(1)}, u32[]{:S(2)}, u32[]{:S(2)}) %collective-permute-start.7) | collective-permute-done | bytes 1048608 | tf_op jit(solution)/shard_map/ppermute | solution.py:42
  82.1 4.7 gather_fusion.5
  90.8 66.4 %all-reduce.5.cloned.1.call-done = f32[256,256]{1,0:T(8,128)} async-done(((f32[256,256]{1,0:T(8,128)}), f32[256,256]{1,0:T(8,128)}) %all-reduce.5.cloned.1.call-update) | async-done | bytes 262160 | tf_op jit(solution)/shard_map/psum | solution.py:102
  160.4 149.8 %all-reduce.7.cloned.1.call-done = f32[1024,256]{0,1:T(8,128)} async-done(((f32[1024,256]{0,1:T(8,128)}), f32[1024,256]{0,1:T(8,128)}) %all-reduce.7.cloned.1.call-update) | async-done | bytes 1048592 | tf_op jit(solution)/shard_map/psum | solution.py:104
  347.7 6.9 fusion.12
  356.2 4.7 gather_fusion.6
  368.1 4.7 collective-permute-done.16
  372.8 4.7 collective-permute-done.15
  377.8 4.0 collective-permute-start.17
  383.8 19.3 %collective-permute-done.17 = f32[4,1,256,256]{3,2,1,0:T(8,128)S(1)} collective-permute-done((f32[4,1,256,256]{3,2,1,0:T(8,128)S(1)}, f32[4,1,256,256]{3,2,1,0:T(8,128)S(1)}, u32[]{:S(2)}, u32[]{:S(2)}) %collective-permute-start.17) | collective-permute-done | bytes 1048608 | tf_op jit(solution)/shard_map/ppermute | solution.py:41
  403.1 5.8 collective-permute-done.18
  409.0 4.7 gather_fusion.7
  416.3 6.4 fusion.27
  423.1 4.7 gather_fusion.8
  433.7 4.2 collective-permute-done.20
  444.0 4.1 collective-permute-start.22
  448.2 19.7 %collective-permute-done.21 = f32[4,1,256,256]{3,2,1,0:T(8,128)S(1)} collective-permute-done((f32[4,1,256,256]{3,2,1,0:T(8,128)S(1)}, f32[4,1,256,256]{3,2,1,0:T(8,128)S(1)}, u32[]{:S(2)}, u32[]{:S(2)}) %collective-permute-start.21) | collective-permute-done | bytes 1048608 | tf_op jit(solution)/shard_map/ppermute | solution.py:41
  467.9 4.0 collective-permute-done.22
  472.0 4.7 gather_fusion.9
  480.7 62.7 %all-reduce.9.cloned.1.call-done = f32[256,256]{1,0:T(8,128)} async-done(((f32[256,256]{1,0:T(8,128)}), f32[256,256]{1,0:T(8,128)}) %all-reduce.9.cloned.1.call-update) | async-done | bytes 262160 | tf_op jit(solution)/shard_map/psum | solution.py:102
  546.3 149.5 %all-reduce.11.cloned.1.call-done = f32[1024,256]{0,1:T(8,128)} async-done(((f32[1024,256]{0,1:T(8,128)}), f32[1024,256]{0,1:T(8,128)}) %all-reduce.11.cloned.1.call-update) | async-done | bytes 1048592 | tf_op jit(solution)/shard_map/psum | solution.py:104
  732.1 7.0 fusion.21
  750.0 4.7 collective-permute-done.31
  754.7 4.7 collective-permute-done.30
  759.7 4.0 collective-permute-start.32
  765.7 19.3 %collective-permute-done.32 = f32[4,1,256,256]{3,2,1,0:T(8,128)S(1)} collective-permute-done((f32[4,1,256,256]{3,2,1,0:T(8,128)S(1)}, f32[4,1,256,256]{3,2,1,0:T(8,128)S(1)}, u32[]{:S(2)}, u32[]{:S(2)}) %collective-permute-start.32) | collective-permute-done | bytes 1048608 | tf_op jit(solution)/shard_map/ppermute | solution.py:41
  785.0 5.8 collective-permute-done.33
  790.9 4.7 gather_fusion.11
  (218 shorter events, 172.6 us)
Async XLA Ops:
  6.5 150.6 %all-reduce.5.cloned.1.call-start = ((), (), s32[]{:S(2)}) async-start(), calls=%async_computation | async-start | bytes 524288 | tf_op jit(solution)/shard_map/psum | solution.py:102
  17.7 15.2 %collective-permute-start.1 = (f32[1,2,256,1]{2,1,3,0:T(2,128)S(1)}, f32[1,2,256,1]{2,1,3,0:T(2,128)S(1)}, u32[]{:S(2)}, u32[]{:S(2)}) collective-permute-start(f32[1,2,256,1]{2,1,3,0:T(2,128)S(1)} %maximum_bitcast_fusion.9), channel_id=1, source_target_pairs={{32,0},{64,32},{96,64},{128,96},{160,128},{192,160},{224,192},{33,... | collective-permute-start | bytes 6152 | tf_op jit(solution)/shard_map/ppermute | solution.py:42
  19.6 13.3 %collective-permute-start = (f32[1,2,256,1]{2,1,3,0:T(2,128)S(1)}, f32[1,2,256,1]{2,1,3,0:T(2,128)S(1)}, u32[]{:S(2)}, u32[]{:S(2)}) collective-permute-start(f32[1,2,256,1]{2,1,3,0:T(2,128)S(1)} %maximum_bitcast_fusion.8), channel_id=1, source_target_pairs={{0,32},{32,64},{64,96},{96,128},{128,160},{160,192},{192,224},{1,3... | collective-permute-start | bytes 6152 | tf_op jit(solution)/shard_map/ppermute | solution.py:41
  26.6 12.2 %collective-permute-start.5 = (f32[1,2,256,256]{3,2,1,0:T(8,128)}, f32[1,2,256,256]{3,2,1,0:T(8,128)}, u32[]{:S(2)}, u32[]{:S(2)}) collective-permute-start(f32[1,2,256,256]{3,2,1,0:T(8,128)} %maximum_bitcast_fusion.1), channel_id=1, source_target_pairs={{32,0},{64,32},{96,64},{128,96},{160,128},{192,160},{224,192},{33,... | collective-permute-start | bytes 1572872 | tf_op jit(solution)/shard_map/ppermute | solution.py:42
  30.6 10.8 %collective-permute-start.4 = (f32[1,2,256,256]{3,2,1,0:T(8,128)}, f32[1,2,256,256]{3,2,1,0:T(8,128)}, u32[]{:S(2)}, u32[]{:S(2)}) collective-permute-start(f32[1,2,256,256]{3,2,1,0:T(8,128)} %maximum_bitcast_fusion), channel_id=1, source_target_pairs={{0,32},{32,64},{64,96},{96,128},{128,160},{160,192},{192,224},{1,3... | collective-permute-start | bytes 1572872 | tf_op jit(solution)/shard_map/ppermute | solution.py:41
  32.9 5.9 collective-permute-start.2
  36.7 11.3 %collective-permute-start.3 = (f32[4,1,256,1]{2,1,3,0:T(1,128)S(1)}, f32[4,1,256,1]{2,1,3,0:T(1,128)S(1)}, u32[]{:S(2)}, u32[]{:S(2)}) collective-permute-start(f32[4,1,256,1]{2,1,3,0:T(1,128)S(1)} %get-tuple-element.38), channel_id=1, source_target_pairs={{1,0},{2,1},{3,2},{4,3},{5,4},{6,5},{7,6},{8,7},{9,8},{10,9},{11,1... | collective-permute-start | bytes 12296 | tf_op jit(solution)/shard_map/ppermute | solution.py:42
  44.2 27.3 %collective-permute-start.6 = (f32[4,1,256,256]{3,2,1,0:T(8,128)}, f32[4,1,256,256]{3,2,1,0:T(8,128)}, u32[]{:S(2)}, u32[]{:S(2)}) collective-permute-start(f32[4,1,256,256]{3,2,1,0:T(8,128)} %get-tuple-element.19), channel_id=1, source_target_pairs={{0,1},{1,2},{2,3},{3,4},{4,5},{5,6},{6,7},{7,8},{8,9},{9,10},{10,1... | collective-permute-start | bytes 3145736 | tf_op jit(solution)/shard_map/ppermute | solution.py:41
  52.5 29.4 %collective-permute-start.7 = (f32[4,1,256,256]{3,2,1,0:T(8,128)S(1)}, f32[4,1,256,256]{3,2,1,0:T(8,128)S(1)}, u32[]{:S(2)}, u32[]{:S(2)}) collective-permute-start(f32[4,1,256,256]{3,2,1,0:T(8,128)S(1)} %get-tuple-element.20), channel_id=1, source_target_pairs={{1,0},{2,1},{3,2},{4,3},{5,4},{6,5},{7,6},{8,7},{9,8},{10,9},{11,1... | collective-permute-start | bytes 3145736 | tf_op jit(solution)/shard_map/ppermute | solution.py:42
  90.7 219.5 %all-reduce.7.cloned.1.call-start = ((), (), s32[]{:S(2)}) async-start(), calls=%async_computation.1 | async-start | bytes 2097152 | tf_op jit(solution)/shard_map/psum | solution.py:104
  160.2 383.2 %all-reduce.9.cloned.1.call-start = ((), (), s32[]{:S(2)}) async-start(), calls=%async_computation.2 | async-start | bytes 524288 | tf_op jit(solution)/shard_map/psum | solution.py:102
  311.2 4.5 collective-permute-start.8
  315.7 4.7 collective-permute-start.9
  315.7 4.7 collective-permute-start.13
  320.5 4.7 collective-permute-start.10
  320.5 10.5 %collective-permute-start.14 = (f32[32,256]{0,1:T(8,128)}, f32[32,256]{0,1:T(8,128)}, u32[]{:S(2)}, u32[]{:S(2)}) collective-permute-start(f32[32,256]{0,1:T(8,128)} %collective-permute-done.13), channel_id=1, source_target_pairs={{32,0},{64,32},{96,64},{128,96},{160,128},{192,160},{224,192},{0,2... | collective-permute-start | bytes 98312 | tf_op jit(solution)/shard_map/ppermute | solution.py:27
  325.2 8.4 %collective-permute-start.11 = (f32[32,256]{0,1:T(8,128)}, f32[32,256]{0,1:T(8,128)}, u32[]{:S(2)}, u32[]{:S(2)}) collective-permute-start(f32[32,256]{0,1:T(8,128)} %collective-permute-done.10), channel_id=1, source_target_pairs={{0,32},{32,64},{64,96},{96,128},{128,160},{160,192},{192,224},{224... | collective-permute-start | bytes 98312 | tf_op jit(solution)/shard_map/ppermute | solution.py:25
  362.5 10.3 %collective-permute-start.16 = (f32[1,2,256,256]{3,2,1,0:T(8,128)S(1)}, f32[1,2,256,256]{3,2,1,0:T(8,128)S(1)}, u32[]{:S(2)}, u32[]{:S(2)}) collective-permute-start(f32[1,2,256,256]{3,2,1,0:T(8,128)S(1)} %maximum_bitcast_fusion.3), channel_id=1, source_target_pairs={{32,0},{64,32},{96,64},{128,96},{160,128},{192,160},{224,192},{33,... | collective-permute-start | bytes 1572872 | tf_op jit(solution)/shard_map/ppermute | solution.py:42
  366.2 11.3 %collective-permute-start.15 = (f32[1,2,256,256]{3,2,1,0:T(8,128)S(1)}, f32[1,2,256,256]{3,2,1,0:T(8,128)S(1)}, u32[]{:S(2)}, u32[]{:S(2)}) collective-permute-start(f32[1,2,256,256]{3,2,1,0:T(8,128)S(1)} %maximum_bitcast_fusion.2), channel_id=1, source_target_pairs={{0,32},{32,64},{64,96},{96,128},{128,160},{160,192},{192,224},{1,3... | collective-permute-start | bytes 1572872 | tf_op jit(solution)/shard_map/ppermute | solution.py:41
  377.8 25.3 %collective-permute-start.17 = (f32[4,1,256,256]{3,2,1,0:T(8,128)S(1)}, f32[4,1,256,256]{3,2,1,0:T(8,128)S(1)}, u32[]{:S(2)}, u32[]{:S(2)}) collective-permute-start(f32[4,1,256,256]{3,2,1,0:T(8,128)S(1)} %get-tuple-element.17), channel_id=1, source_target_pairs={{0,1},{1,2},{2,3},{3,4},{4,5},{5,6},{6,7},{7,8},{8,9},{9,10},{10,1... | collective-permute-start | bytes 3145736 | tf_op jit(solution)/shard_map/ppermute | solution.py:41
  381.8 27.1 %collective-permute-start.18 = (f32[4,1,256,256]{3,2,1,0:T(8,128)S(1)}, f32[4,1,256,256]{3,2,1,0:T(8,128)S(1)}, u32[]{:S(2)}, u32[]{:S(2)}) collective-permute-start(f32[4,1,256,256]{3,2,1,0:T(8,128)S(1)} %get-tuple-element.18), channel_id=1, source_target_pairs={{1,0},{2,1},{3,2},{4,3},{5,4},{6,5},{7,6},{8,7},{9,8},{10,9},{11,1... | collective-permute-start | bytes 3145736 | tf_op jit(solution)/shard_map/ppermute | solution.py:42
  429.3 8.6 %collective-permute-start.20 = (f32[1,2,256,256]{3,2,1,0:T(8,128)S(1)}, f32[1,2,256,256]{3,2,1,0:T(8,128)S(1)}, u32[]{:S(2)}, u32[]{:S(2)}) collective-permute-start(f32[1,2,256,256]{3,2,1,0:T(8,128)S(1)} %maximum_bitcast_fusion.5), channel_id=1, source_target_pairs={{32,0},{64,32},{96,64},{128,96},{160,128},{192,160},{224,192},{33,... | collective-permute-start | bytes 1572872 | tf_op jit(solution)/shard_map/ppermute | solution.py:42
  431.3 10.5 %collective-permute-start.19 = (f32[1,2,256,256]{3,2,1,0:T(8,128)S(1)}, f32[1,2,256,256]{3,2,1,0:T(8,128)S(1)}, u32[]{:S(2)}, u32[]{:S(2)}) collective-permute-start(f32[1,2,256,256]{3,2,1,0:T(8,128)S(1)} %maximum_bitcast_fusion.4), channel_id=1, source_target_pairs={{0,32},{32,64},{64,96},{96,128},{128,160},{160,192},{192,224},{1,3... | collective-permute-start | bytes 1572872 | tf_op jit(solution)/shard_map/ppermute | solution.py:41
  442.1 25.8 %collective-permute-start.21 = (f32[4,1,256,256]{3,2,1,0:T(8,128)S(1)}, f32[4,1,256,256]{3,2,1,0:T(8,128)S(1)}, u32[]{:S(2)}, u32[]{:S(2)}) collective-permute-start(f32[4,1,256,256]{3,2,1,0:T(8,128)S(1)} %get-tuple-element.15), channel_id=1, source_target_pairs={{0,1},{1,2},{2,3},{3,4},{4,5},{5,6},{6,7},{7,8},{8,9},{9,10},{10,1... | collective-permute-start | bytes 3145736 | tf_op jit(solution)/shard_map/ppermute | solution.py:41
  444.0 27.9 %collective-permute-start.22 = (f32[4,1,256,256]{3,2,1,0:T(8,128)S(1)}, f32[4,1,256,256]{3,2,1,0:T(8,128)S(1)}, u32[]{:S(2)}, u32[]{:S(2)}) collective-permute-start(f32[4,1,256,256]{3,2,1,0:T(8,128)S(1)} %get-tuple-element.16), channel_id=1, source_target_pairs={{1,0},{2,1},{3,2},{4,3},{5,4},{6,5},{7,6},{8,7},{9,8},{10,9},{11,1... | collective-permute-start | bytes 3145736 | tf_op jit(solution)/shard_map/ppermute | solution.py:42
  480.6 215.2 %all-reduce.11.cloned.1.call-start = ((), (), s32[]{:S(2)}) async-start(), calls=%async_computation.3 | async-start | bytes 2097152 | tf_op jit(solution)/shard_map/psum | solution.py:104
  706.3 9.1 %collective-permute-start.29 = (f32[32,256]{0,1:T(8,128)}, f32[32,256]{0,1:T(8,128)}, u32[]{:S(2)}, u32[]{:S(2)}) collective-permute-start(f32[32,256]{0,1:T(8,128)} %collective-permute-done.28), channel_id=1, source_target_pairs={{32,0},{64,32},{96,64},{128,96},{160,128},{192,160},{224,192},{0,2... | collective-permute-start | bytes 98312 | tf_op jit(solution)/shard_map/ppermute | solution.py:27
  710.1 7.8 collective-permute-start.26
  744.4 10.3 %collective-permute-start.31 = (f32[1,2,256,256]{3,2,1,0:T(8,128)S(1)}, f32[1,2,256,256]{3,2,1,0:T(8,128)S(1)}, u32[]{:S(2)}, u32[]{:S(2)}) collective-permute-start(f32[1,2,256,256]{3,2,1,0:T(8,128)S(1)} %maximum_bitcast_fusion.7), channel_id=1, source_target_pairs={{32,0},{64,32},{96,64},{128,96},{160,128},{192,160},{224,192},{33,... | collective-permute-start | bytes 1572872 | tf_op jit(solution)/shard_map/ppermute | solution.py:42
  748.1 11.3 %collective-permute-start.30 = (f32[1,2,256,256]{3,2,1,0:T(8,128)S(1)}, f32[1,2,256,256]{3,2,1,0:T(8,128)S(1)}, u32[]{:S(2)}, u32[]{:S(2)}) collective-permute-start(f32[1,2,256,256]{3,2,1,0:T(8,128)S(1)} %maximum_bitcast_fusion.6), channel_id=1, source_target_pairs={{0,32},{32,64},{64,96},{96,128},{128,160},{160,192},{192,224},{1,3... | collective-permute-start | bytes 1572872 | tf_op jit(solution)/shard_map/ppermute | solution.py:41
  759.7 25.3 %collective-permute-start.32 = (f32[4,1,256,256]{3,2,1,0:T(8,128)S(1)}, f32[4,1,256,256]{3,2,1,0:T(8,128)S(1)}, u32[]{:S(2)}, u32[]{:S(2)}) collective-permute-start(f32[4,1,256,256]{3,2,1,0:T(8,128)S(1)} %get-tuple-element.13), channel_id=1, source_target_pairs={{0,1},{1,2},{2,3},{3,4},{4,5},{5,6},{6,7},{7,8},{8,9},{9,10},{10,1... | collective-permute-start | bytes 3145736 | tf_op jit(solution)/shard_map/ppermute | solution.py:41
  763.7 27.1 %collective-permute-start.33 = (f32[4,1,256,256]{3,2,1,0:T(8,128)S(1)}, f32[4,1,256,256]{3,2,1,0:T(8,128)S(1)}, u32[]{:S(2)}, u32[]{:S(2)}) collective-permute-start(f32[4,1,256,256]{3,2,1,0:T(8,128)S(1)} %get-tuple-element.14), channel_id=1, source_target_pairs={{1,0},{2,1},{3,2},{4,3},{5,4},{6,5},{7,6},{8,7},{9,8},{10,9},{11,1... | collective-permute-start | bytes 3145736 | tf_op jit(solution)/shard_map/ppermute | solution.py:42
  (23 other events, 275.3 us)
Sparse Core Ops, SparseCore 0:
  90.8 66.3 all-reduce.4
  161.0 149.1 all-reduce.6
  480.7 62.5 all-reduce.8
  546.6 149.1 all-reduce.10
